TPU v7x, 256 devices: a whole 4x4x8 slice. The times are simulated.
256 devices in a mesh: blk: 8 (over z_lo, core), wide: 32 (over x, z_hi, y).
Axes of the slice: x: 4, y: 4, z: 8 (z_hi: 2, z_lo: 4; z = z_hi * 4 + z_lo), core: 2. Of those that a mesh axis runs over, the one named last changes fastest.
Arguments:
- surf_xyz: float32 [3, 131072], P(None, ('blk', 'wide')), may hold values from -5 to 5
- surf_disp: float32 [24, 131072], P(None, ('blk', 'wide')), may hold values from -12 to 12
- neighbours: int32 [4, 131072], P(None, ('blk', 'wide')), may hold values from 0 to 16383, as said below
- vol_xyz: float32 [3, 65536], P(None, ('blk', 'wide')), may hold values from -4 to 4
Outputs:
- displacement: float32 [24, 65536], P(None, ('blk', 'wide'))
Inputs may be any that keep to these rules, and one draw needn't show every extreme that they name: `neighbours`: column j names surface nodes of the same group of 16384 consecutive nodes as j, by their index within that group; every group is a renumbering of square patches of 16 x 16 nodes.
All inputs are finite; a program needn't handle non-finite values.
Results may differ from a plain program's by a relative error of at most 0.012.
The roundings to bfloat16 on the way count: a program that leaves them out, or rounds other values in their place, can miss the bound.
Values may be sent and summed in bfloat16 or wider, within the bound.
A program may use at most 64 MiB of HBM per device.

v0:
```python
import math

import jax
import jax.numpy as jnp
from jax import lax
from jax.sharding import PartitionSpec as P

tangent_floor = 0.04
core_radius = 0.04


def from_behind(shard, axis, by):
    peers = lax.axis_size(axis)
    return lax.ppermute(shard, axis, [(i, (i + by) % peers) for i in range(peers)])


def form_blocks(source_xyz, source_disp, links, node_xyz, node_disp):
    count = links.shape[1]
    cases = node_disp.shape[0] // 3
    tangent_one = jnp.take(source_xyz, links[0], axis=1) - jnp.take(source_xyz, links[1], axis=1)
    tangent_two = jnp.take(source_xyz, links[2], axis=1) - jnp.take(source_xyz, links[3], axis=1)
    change_one = (
        jnp.take(source_disp, links[0], axis=1) - jnp.take(source_disp, links[1], axis=1)
    ).reshape(cases, 3, count)
    change_two = (
        jnp.take(source_disp, links[2], axis=1) - jnp.take(source_disp, links[3], axis=1)
    ).reshape(cases, 3, count)
    length_one = (
        tangent_one[0] * tangent_one[0]
        + tangent_one[1] * tangent_one[1]
        + tangent_one[2] * tangent_one[2]
    )
    length_two = (
        tangent_two[0] * tangent_two[0]
        + tangent_two[1] * tangent_two[1]
        + tangent_two[2] * tangent_two[2]
    )
    scaled_one = tangent_one / (length_one + tangent_floor)
    scaled_two = tangent_two / (length_two + tangent_floor)
    linear = (
        change_one[:, :, None, :] * scaled_one[None, None, :, :]
        + change_two[:, :, None, :] * scaled_two[None, None, :, :]
    )
    moved = node_disp.reshape(cases, 3, count)
    offset = (
        linear[:, :, 0, :] * node_xyz[0]
        + linear[:, :, 1, :] * node_xyz[1]
        + linear[:, :, 2, :] * node_xyz[2]
    )
    blocks = jnp.concatenate([linear.reshape(cases, 9, count), moved - offset], axis=1)
    return blocks.reshape(cases * 12, count).astype(jnp.bfloat16)


def pair_weights(source_xyz, target_xyz):
    delta_x = source_xyz[0][:, None] - target_xyz[0][None, :]
    delta_y = source_xyz[1][:, None] - target_xyz[1][None, :]
    delta_z = source_xyz[2][:, None] - target_xyz[2][None, :]
    radius = delta_x * delta_x + delta_y * delta_y + delta_z * delta_z + core_radius
    return (1.0 / (radius * radius)).astype(jnp.bfloat16)


def finish(numerator, denominator, target_xyz):
    cases = numerator.shape[0] // 12
    count = numerator.shape[1]
    grouped = numerator.reshape(cases, 12, count)
    linear = grouped[:, :9].reshape(cases, 3, 3, count)
    moved = (
        linear[:, :, 0] * target_xyz[0]
        + linear[:, :, 1] * target_xyz[1]
        + linear[:, :, 2] * target_xyz[2]
        + grouped[:, 9:]
    )
    return (moved / denominator).reshape(cases * 3, count)


def accumulate(blocks, group_xyz, target_xyz, numerator, denominator):
    count = blocks.shape[1]
    width = math.gcd(1024, count)

    def one_piece(index, carry):
        partial_num, partial_den = carry
        start = index * width
        block_piece = lax.dynamic_slice_in_dim(blocks, start, width, 1)
        source_piece = lax.dynamic_slice_in_dim(group_xyz, start, width, 1)
        weights = pair_weights(source_piece, target_xyz)
        partial_num = partial_num + jnp.dot(
            block_piece, weights, preferred_element_type=jnp.float32
        )
        partial_den = partial_den + jnp.sum(weights.astype(jnp.float32), axis=0)
        return (partial_num, partial_den)

    return lax.fori_loop(0, count // width, one_piece, (numerator, denominator))


def on_device(surf_xyz, surf_disp, neighbours, vol_xyz):
    group_xyz, group_disp = (
        lax.all_gather(surf_xyz, "wide", axis=1, tiled=True),
        lax.all_gather(surf_disp, "wide", axis=1, tiled=True),
    )
    own_blocks = form_blocks(group_xyz, group_disp, neighbours, surf_xyz, surf_disp)
    blocks = lax.all_gather(own_blocks, "wide", axis=1, tiled=True)
    rows = blocks.shape[0]
    volume = vol_xyz.shape[1]
    groups = lax.axis_size("blk")
    visit_xyz = vol_xyz
    numerator = jnp.zeros((rows, volume), jnp.float32)
    denominator = jnp.zeros((volume,), jnp.float32)
    for step in range(groups):
        numerator, denominator = accumulate(blocks, group_xyz, visit_xyz, numerator, denominator)
        visit_xyz, numerator, denominator = from_behind(
            (visit_xyz, numerator, denominator), "blk", 1
        )
    return finish(numerator, denominator, vol_xyz)


def solution(mesh):
    in_specs = (
        P(None, ("blk", "wide")),
        P(None, ("blk", "wide")),
        P(None, ("blk", "wide")),
        P(None, ("blk", "wide")),
    )
    out_specs = P(None, ("blk", "wide"))
    return jax.shard_map(
        on_device, mesh=mesh, in_specs=in_specs, out_specs=out_specs, check_vma=False
    )
```

profile of v0, /device:TPU:1, one launch (start us, length us, event | category | flops | bytes accessed | tf_op | source)
XLA Modules:
  0.0 804.5 jit_solution(5151948245214430202)
XLA Ops:
  6.5 1.6 copy.76
  10.0 287.9 %all_gather.10 = f32[3,16384]{0,1:T(8,128)} all-gather(f32[3,512]{0,1:T(8,128)S(1)} %copy.80), channel_id=1, replica_groups=mesh['blk'=8,'wide'=32] {'wide'}, dimensions={1}, use_global_device_ids=true | all-gather | bytes 202752 | tf_op jit(solution)/shard_map/all_gather | solution.py:97
  298.0 4.4 gather_fusion.7
  302.5 4.4 gather_fusion.6
  307.2 4.4 gather_fusion.3
  311.7 4.4 gather_fusion.2
  316.4 4.4 gather_fusion.5
  320.8 4.4 gather_fusion.4
  325.6 4.4 gather_fusion.1
  330.0 4.4 gather_fusion
  335.7 5.5 copy.90
  341.2 126.0 %all-gather.5.cloned.1.call-done = bf16[96,16384]{1,0:T(8,128)(2,1)} async-done(((bf16[96,512]{1,0:T(8,128)(2,1)}), bf16[96,16384]{1,0:T(8,128)(2,1)}) %all-gather.5.cloned.1.call-update) | async-done | bytes 3145744 | tf_op jit(solution)/shard_map/all_gather | solution.py:101
  467.1 35.8 %while.128 = (s32[]{:T(128)}, f32[96,256]{1,0:T(8,128)S(1)}, f32[256]{0:T(256)S(1)}, bf16[96,16384]{1,0:T(8,128)(2,1)}, f32[3,16384]{1,0:T(4,128)S(1)}, /*index=...) while((s32[]{:T(128)}, f32[96,256]{1,0:T(8,128)S(1)}, ...), condition=%wide.region_2.5_spmd.clone, body=%wide.region_0.4_spmd.clone.sunk | while | flops 57196808 | bytes 458974 | solution.py:92
  467.8 1.6 convolution_add_fusion.23
  470.0 1.6 convolution_add_fusion.23
  472.2 1.6 convolution_add_fusion.23
  474.5 1.6 convolution_add_fusion.23
  476.7 1.6 convolution_add_fusion.23
  479.0 1.6 convolution_add_fusion.23
  481.2 1.6 convolution_add_fusion.23
  483.5 1.6 convolution_add_fusion.23
  485.7 1.6 convolution_add_fusion.23
  487.9 1.6 convolution_add_fusion.23
  490.2 1.6 convolution_add_fusion.23
  492.4 1.6 convolution_add_fusion.23
  494.7 1.6 convolution_add_fusion.23
  496.9 1.6 convolution_add_fusion.23
  499.2 1.6 convolution_add_fusion.23
  501.4 1.6 convolution_add_fusion.23
  503.0 2.4 collective-permute-start
  507.1 35.5 %while.121 = (s32[]{:T(128)}, f32[96,256]{1,0:T(8,128)S(1)}, f32[256]{0:T(256)S(1)}, bf16[96,16384]{1,0:T(8,128)(2,1)}, f32[3,16384]{1,0:T(4,128)S(1)}, /*index=...) while((s32[]{:T(128)}, f32[96,256]{1,0:T(8,128)S(1)}, ...), condition=%wide.region_5.8_spmd, body=%wide.region_3.7_spmd.sunk | while | flops 57171976 | bytes 458955 | solution.py:92
  542.6 2.5 collective-permute-start.3
  545.5 1.9 collective-permute-done.5
  547.7 35.5 %while.122 = (s32[]{:T(128)}, f32[96,256]{1,0:T(8,128)S(1)}, f32[256]{0:T(256)S(1)}, bf16[96,16384]{1,0:T(8,128)(2,1)}, f32[3,16384]{1,0:T(4,128)S(1)}, /*index=...) while((s32[]{:T(128)}, f32[96,256]{1,0:T(8,128)S(1)}, ...), condition=%wide.region_8.11_spmd, body=%wide.region_6.10_spmd.sunk | while | flops 57171976 | bytes 458955 | solution.py:92
  548.3 1.6 convolution_add_fusion.17
  583.2 1.7 collective-permute-start.6
  585.0 2.2 collective-permute-start.7
  587.2 1.8 collective-permute-done.8
  589.1 35.6 %while.123 = (s32[]{:T(128)}, f32[96,256]{1,0:T(8,128)S(1)}, f32[256]{0:T(256)S(1)}, bf16[96,16384]{1,0:T(8,128)(2,1)}, f32[3,16384]{1,0:T(4,128)S(1)}, /*index=...) while((s32[]{:T(128)}, f32[96,256]{1,0:T(8,128)S(1)}, ...), condition=%wide.region_11.14_spmd, body=%wide.region_9.13_spmd.sunk | while | flops 57171976 | bytes 458955 | solution.py:92
  589.7 1.6 convolution_add_fusion.18
  591.9 1.6 convolution_add_fusion.18
  594.1 1.6 convolution_add_fusion.18
  626.5 2.3 collective-permute-start.10
  628.8 1.8 collective-permute-done.11
  630.6 35.6 %while.124 = (s32[]{:T(128)}, f32[96,256]{1,0:T(8,128)S(1)}, f32[256]{0:T(256)S(1)}, bf16[96,16384]{1,0:T(8,128)(2,1)}, f32[3,16384]{1,0:T(4,128)S(1)}, /*index=...) while((s32[]{:T(128)}, f32[96,256]{1,0:T(8,128)S(1)}, ...), condition=%wide.region_14.17_spmd, body=%wide.region_12.16_spmd.sunk | while | flops 57171976 | bytes 458955 | solution.py:92
  631.3 1.6 convolution_add_fusion.19
  633.5 1.6 convolution_add_fusion.19
  635.7 1.6 convolution_add_fusion.19
  637.9 1.6 convolution_add_fusion.19
  668.1 2.3 collective-permute-start.13
  670.4 1.8 collective-permute-done.14
  672.2 35.6 %while.125 = (s32[]{:T(128)}, f32[96,256]{1,0:T(8,128)S(1)}, f32[256]{0:T(256)S(1)}, bf16[96,16384]{1,0:T(8,128)(2,1)}, f32[3,16384]{1,0:T(4,128)S(1)}, /*index=...) while((s32[]{:T(128)}, f32[96,256]{1,0:T(8,128)S(1)}, ...), condition=%wide.region_17.20_spmd, body=%wide.region_15.19_spmd.sunk | while | flops 57171976 | bytes 458955 | solution.py:92
  672.8 1.6 convolution_add_fusion.20
  675.0 1.6 convolution_add_fusion.20
  677.3 1.6 convolution_add_fusion.20
  679.5 1.6 convolution_add_fusion.20
  709.7 2.3 collective-permute-start.16
  712.0 1.9 collective-permute-done.17
  714.0 35.5 %while.126 = (s32[]{:T(128)}, f32[96,256]{1,0:T(8,128)S(1)}, f32[256]{0:T(256)S(1)}, bf16[96,16384]{1,0:T(8,128)(2,1)}, f32[3,16384]{1,0:T(4,128)S(1)}, /*index=...) while((s32[]{:T(128)}, f32[96,256]{1,0:T(8,128)S(1)}, ...), condition=%wide.region_20.23_spmd, body=%wide.region_18.22_spmd.sunk | while | flops 57171976 | bytes 458955 | solution.py:92
  714.6 1.6 convolution_add_fusion.21
  751.3 2.3 collective-permute-start.19
  753.5 1.8 collective-permute-done.20
  755.4 35.6 %while.127 = (s32[]{:T(128)}, f32[96,256]{1,0:T(8,128)S(1)}, f32[256]{0:T(256)S(1)}, bf16[96,16384]{1,0:T(8,128)(2,1)}, f32[3,16384]{1,0:T(4,128)S(1)}, /*index=...) while((s32[]{:T(128)}, f32[96,256]{1,0:T(8,128)S(1)}, ...), condition=%wide.region_23.26_spmd, body=%wide.region_21.25_spmd.sunk | while | flops 57171976 | bytes 458955 | solution.py:92
  792.8 4.1 collective-permute-done.21
  (703 shorter events, 250.0 us)
Async XLA Ops:
  6.5 309.9 %all-gather.3.cloned.1.call-start = ((), (), s32[]{:S(2)}) async-start(), calls=%async_computation | async-start | bytes 8650752 | tf_op jit(solution)/shard_map/all_gather | solution.py:98
  8.2 458.9 %all-gather.5.cloned.1.call-start = ((), (), s32[]{:S(2)}) async-start(), calls=%async_computation.1 | async-start | bytes 3244032 | tf_op jit(solution)/shard_map/all_gather | solution.py:101
  10.0 288.0 %copy-start = (f32[24,512]{1,0:T(8,128)S(1)}, f32[24,512]{1,0:T(8,128)}, u32[]{:S(2)}) copy-start(f32[24,512]{1,0:T(8,128)} %param.25) | copy-start | bytes 147460
  10.0 306.4 %copy-start.2 = (f32[3,512]{1,0:T(4,128)S(1)}, f32[3,512]{1,0:T(4,128)}, u32[]{:S(2)}) copy-start(f32[3,512]{1,0:T(4,128)} %param.24) | copy-start | bytes 18436
  335.7 131.4 %copy-start.1 = (f32[3,256]{1,0:T(4,128)S(1)}, f32[3,256]{1,0:T(4,128)}, u32[]{:S(2)}) copy-start(f32[3,256]{1,0:T(4,128)} %param.27) | copy-start | bytes 9220
  503.0 4.1 collective-permute-start
  505.4 1.7 collective-permute-start.2
  505.5 1.6 collective-permute-start.1
  542.6 5.0 collective-permute-start.3
  545.1 2.3 collective-permute-start.5
  545.2 2.4 collective-permute-start.4
  583.2 5.8 collective-permute-start.6
  584.9 4.1 collective-permute-start.8
  585.0 4.0 collective-permute-start.7
  624.6 6.0 collective-permute-start.9
  625.9 4.7 collective-permute-start.11
  626.5 4.1 collective-permute-start.10
  666.2 6.0 collective-permute-start.12
  667.5 4.7 collective-permute-start.14
  668.1 4.1 collective-permute-start.13
  707.8 6.2 collective-permute-start.15
  709.0 4.9 collective-permute-start.17
  709.7 4.3 collective-permute-start.16
  749.6 5.8 collective-permute-start.18
  750.6 4.7 collective-permute-start.20
  751.3 4.1 collective-permute-start.19
  790.9 6.0 collective-permute-start.21
  792.2 4.8 collective-permute-start.22
Sparse Core Ops, SparseCore 0:
  10.9 228.3 all-gather.2
  335.8 131.2 all-gather.4
where the time goes:
time: 811 us; the launch traced here: 804 us
  blocking collectives  288 us (36%)
  matrix products  201 us (25%)
  waiting for transfers between devices  143 us (18%)
  other arithmetic  66.2 us (8%)
  local copies, waits for them, and re-layouts  58.7 us (7%)
  starting transfers between devices  28.1 us (3%)
  between operations  13.9 us (2%)
    all_gather x1, blocking collectives, on_device(): lax.all_gather(surf_xyz, 'wide', axis=1, tiled=True)  288 us
    dot_general x128, matrix products, one_piece(): jnp.dot(block_piece, weights, preferred_element_type=jnp.float32)  201 us
    all_gather x1, waiting for transfers between devices, on_device(): blocks = lax.all_gather(own_blocks, 'wide', axis=1, tiled=True)  126 us
    reduce_sum x128, other arithmetic, one_piece(): partial_den = partial_den + jnp.sum(weights.astype(jnp.float32), axis=0)  64.1 us
    ppermute x23, starting transfers between devices, from_behind(): lax.ppermute(shard, axis, [(i, (i + by) % peers) for i in range(peers)])  28.1 us
    ppermute x23, waiting for transfers between devices, from_behind(): lax.ppermute(shard, axis, [(i, (i + by) % peers) for i in range(peers)])  16.9 us
  transfers between devices with their start and end apart: 25, of which 11 were waited for; matrix products, arithmetic and copies ran while one was open for 3% of the time, Pallas kernels for 0%

commit v1 on v0

v1 whole, which is shorter than its diff:
```python
import jax
import jax.numpy as jnp
from jax import lax
from jax.experimental import pallas as pl
from jax.experimental.pallas import tpu as pltpu
from jax.sharding import PartitionSpec as P

MESH = pl.DeviceIdType.MESH
tangent_floor = 0.04
core_radius = 0.04
f32, bf16, i32 = jnp.float32, jnp.bfloat16, jnp.int32

NX, NY, NZ = 4, 4, 8
LOW = 4
OWN = 512
VOWN = 256
TILE = 512
SET = 8
S_ALL = SET * OWN
V_SLOTS = NX * NZ
V_ALL = V_SLOTS * VOWN
PER_TILE = TILE // VOWN
TILES = V_ALL // TILE
ROWS = 104
FEAT = 32
CACHED = 0


def device(x, y, z, core):
    return (lax.rem(z, LOW) * 2 + core, (x * 2 + lax.div(z, LOW)) * NY + y)


def offsets(slot):
    p, q = slot // NX, slot % NX
    dz = 4 + (1 - 2 * (p % 2)) * ((p + 1) // 2)
    dx = 2 + (1 - 2 * (q % 2)) * ((q + 1) // 2)
    return dx, dz


INVERSE = []
for slot in range(V_SLOTS):
    dx, dz = offsets(slot)
    INVERSE.append(
        [k for k in range(V_SLOTS) if offsets(k) == ((-dx) % NX, (-dz) % NZ)][0]
    )


def split(value):
    high = value.astype(bf16).astype(f32)
    rest = value - high
    middle = rest.astype(bf16).astype(f32)
    return high, middle, (rest - middle).astype(bf16).astype(f32)


PAIRS = ((0, 0), (0, 1), (1, 0), (0, 2), (2, 0), (1, 1), (1, 2), (2, 1))


def feature_rows(xyz, surface):
    count = xyz.shape[1]
    ones = jnp.ones((1, count), f32)
    rows = []
    scale = 1.0 if surface else -2.0
    norm = (xyz[0:1] * xyz[0:1] + xyz[1:2] * xyz[1:2]) + xyz[2:3] * xyz[2:3]
    for axis in range(3):
        parts = split(xyz[axis : axis + 1] * scale)
        rows += [parts[pair[0] if surface else pair[1]] for pair in PAIRS]
    if surface:
        rows += list(split(norm + core_radius)) + [ones] * 3
    else:
        rows += [ones] * 3 + list(split(norm))
    rows += [jnp.zeros((1, count), f32)] * (FEAT - len(rows))
    return jnp.concatenate(rows, axis=0)


def kernel(
    xyz_ref, disp_ref, near_ref, vol_ref, out_ref,
    tab, own_xyz, set_xyz, own_vol, vols, fs, fv, picked, near_rows, near_smem,
    own_blk, blk, part, got, cache,
    z_send, z_recv, x_send, y_send, chunk_recv, sx_send, sx_recv, v_send, v_recv,
    b_send, b_recv, r_send, r_recv, local_sem,
):
    blk_id, wide_id = lax.axis_index("blk"), lax.axis_index("wide")
    core = lax.rem(blk_id, 2)
    z_low = lax.div(blk_id, 2)
    y = lax.rem(wide_id, NY)
    z_high = lax.rem(lax.div(wide_id, NY), 2)
    x = lax.div(wide_id, NY * 2)
    z = z_high * LOW + z_low
    other = 1 - core
    wide_at = lambda ax, ah, ay: (ax * 2 + ah) * NY + ay
    xs = [lax.rem(x + d, NX) for d in range(NX)]
    ys = [lax.rem(y + d, NY) for d in range(NY)]
    far_z = lax.rem(z + LOW, NZ)
    far_h = 1 - z_high

    barrier = pltpu.get_barrier_semaphore()
    peers = []
    for slot in range(V_SLOTS - 1):
        dx, dz = offsets(slot)
        peers.append(device(lax.rem(x + dx, NX), y, lax.rem(z + dz, NZ), core))
    for d in range(1, NY):
        peers.append(device(x, ys[d], z, core))
    for d in range(NY):
        peers.append(device(x, ys[d], z, other))
    for peer in peers:
        pl.semaphore_signal(barrier, inc=1, device_id=peer, device_id_type=MESH)

    xyz = xyz_ref[...]
    disp = disp_ref[...]
    zeros5 = jnp.zeros((5, OWN), f32)
    table = jnp.concatenate([disp, xyz, zeros5], axis=0)
    stacked = jnp.concatenate(
        [table[:, q * 128 : (q + 1) * 128] for q in range(4)], axis=0
    )
    tab[wide_id] = stacked.T
    own_xyz[0:3, :] = xyz
    own_vol[0:3, :] = vol_ref[...]
    near = near_ref[...]
    near_rows[...] = (near // OWN) * 128 + (near & 127)
    to_smem = pltpu.make_async_copy(near_rows, near_smem, local_sem)

    pl.semaphore_wait(barrier, len(peers))
    to_smem.start()

    pending = []

    def send(src, dst, send_sem, recv_sem, peer):
        copy = pltpu.make_async_remote_copy(
            src_ref=src, dst_ref=dst, send_sem=send_sem, recv_sem=recv_sem,
            device_id=peer, device_id_type=MESH,
        )
        copy.start()
        pending.append(copy)

    half = lambda w, h: tab.at[w, pl.ds(h * 64, 64), :]

    def landed(ref, sem):
        pltpu.make_async_copy(ref, ref, sem).wait()

    def send_x(w, h, number):
        for d in range(1, NX):
            send(half(w, h), half(w, h), x_send.at[number, d], chunk_recv.at[w, h],
                 device(xs[d], y, z, core))

    def send_y(w, h, number):
        for d in range(1, NY):
            send(half(w, h), half(w, h), y_send.at[number, d], chunk_recv.at[w, h],
                 device(x, ys[d], z, core))

    far_peer = device(x, y, far_z, core)
    for h in range(2):
        send(half(wide_id, h), half(wide_id, h), z_send.at[h],
             chunk_recv.at[wide_id, h], far_peer)
    send_x(wide_id, 0, 0)
    send_y(wide_id, 1, 0)
    member = core * NY + y
    for c in range(2):
        for d in range(NY):
            if c == 0 and d == 0:
                continue
            send(own_xyz, set_xyz.at[member], sx_send.at[c, d], sx_recv.at[member],
                 device(x, ys[d], z, core if c == 0 else other))
    for slot in range(V_SLOTS - 1):
        dx, dz = offsets(slot)
        send(own_vol, vols.at[INVERSE[slot]], v_send.at[slot],
             v_recv.at[INVERSE[slot]],
             device(lax.rem(x + dx, NX), y, lax.rem(z + dz, NZ), core))

    far_w = wide_at(x, far_h, y)
    for h in range(2):
        landed(half(far_w, h), chunk_recv.at[far_w, h])
    send_x(far_w, 0, 1)
    send_y(far_w, 1, 1)
    number_a = number_b = 0
    send_y(wide_id, 0, 2)
    send_y(far_w, 0, 3)
    send_x(wide_id, 1, 2)
    send_x(far_w, 1, 3)
    number = 4
    for d in range(1, NX):
        for high in (z_high, far_h):
            w = wide_at(xs[d], high, y)
            landed(half(w, 0), chunk_recv.at[w, 0])
            send_y(w, 0, number)
            w = wide_at(x, high, ys[d])
            landed(half(w, 1), chunk_recv.at[w, 1])
            send_x(w, 1, number)
            number += 1

    set_xyz[member] = own_xyz[...]
    vols[V_SLOTS - 1] = own_vol[...]
    for c in range(2):
        for d in range(NY):
            who = (core if c == 0 else other) * NY + ys[d]
            if c or d:
                landed(set_xyz.at[who], sx_recv.at[who])
            rows = feature_rows(set_xyz[who], True)
            at = pl.multiple_of(who * OWN, OWN)
            fs[pl.ds(at, OWN), :] = rows.T.astype(bf16)
    for slot in range(V_SLOTS):
        if slot < V_SLOTS - 1:
            landed(vols.at[slot], v_recv.at[slot])
        fv[:, slot * VOWN : (slot + 1) * VOWN] = feature_rows(
            vols[slot], False
        ).astype(bf16)

    for d in range(1, NX):
        for e in range(1, NY):
            for high in (z_high, far_h):
                w = wide_at(xs[d], high, ys[e])
                for h in range(2):
                    landed(half(w, h), chunk_recv.at[w, h])
    for d in range(1, NX):
        for high in (z_high, far_h):
            w = wide_at(xs[d], high, y)
            landed(half(w, 1), chunk_recv.at[w, 1])
            w = wide_at(x, high, ys[d])
            landed(half(w, 0), chunk_recv.at[w, 0])

    to_smem.wait()
    STEP = 8

    def pick(group, _):
        for k in range(STEP):
            j = group * STEP + k
            for n in range(4):
                row = near_smem[n, j]
                picked[n, pl.ds(j, 1), :] = tab[lax.div(row, 128), pl.ds(lax.rem(row, 128), 1), :]
        return 0

    lax.fori_loop(0, OWN // STEP, pick, 0)
    chosen = []
    for n in range(4):
        quarter = lax.rem(lax.div(near[n : n + 1], 128), 4)
        turned = picked[n].T
        value = turned[0:32]
        for q in range(1, 4):
            value = jnp.where(quarter == q, turned[q * 32 : (q + 1) * 32], value)
        chosen.append(value)
    first, second = chosen[0] - chosen[1], chosen[2] - chosen[3]

    def scaled(change):
        t = change[24:27]
        length = (t[0:1] * t[0:1] + t[1:2] * t[1:2]) + t[2:3] * t[2:3]
        return t / (length + tangent_floor)

    one, two = scaled(first), scaled(second)
    linear = [
        first[0:24] * one[q : q + 1] + second[0:24] * two[q : q + 1] for q in range(3)
    ]
    offset = (linear[0] * xyz[0:1] + linear[1] * xyz[1:2]) + linear[2] * xyz[2:3]
    tail = jnp.where(lax.broadcasted_iota(i32, (8, OWN), 0) == 0, 1.0, 0.0)
    own_blk[...] = jnp.concatenate(linear + [disp - offset, tail], axis=0).astype(bf16)

    def columns(who):
        return blk.at[:, pl.ds(pl.multiple_of(who * OWN, OWN), OWN)]

    own_copy = pltpu.make_async_copy(own_blk, columns(member), local_sem)
    own_copy.start()
    for d in range(1, NY):
        send(own_blk, columns(member), b_send.at[d], b_recv.at[member],
             device(x, ys[d], z, core))
    send(own_blk, columns(member), b_send.at[0], b_recv.at[member],
         device(x, y, z, other))
    own_copy.wait()
    for d in (1, 3, 2):
        who = core * NY + ys[d]
        landed(columns(who), b_recv.at[who])
        send(columns(who), columns(who), b_send.at[3 + d], b_recv.at[who],
             device(x, y, z, other))
    for d in range(NY):
        who = other * NY + ys[d]
        landed(columns(who), b_recv.at[who])

    def weights(tile):
        at = pl.multiple_of(tile * TILE, TILE)
        radius = jnp.dot(fs[...], fv[:, pl.ds(at, TILE)], preferred_element_type=f32)
        return (1.0 / (radius * radius)).astype(bf16)

    def reduce_copy(slot):
        p, q = lax.div(slot, NX), lax.rem(slot, NX)
        dz = 4 + (1 - 2 * lax.rem(p, 2)) * lax.div(p + 1, 2)
        dx = 2 + (1 - 2 * lax.rem(q, 2)) * lax.div(q + 1, 2)
        ip = jnp.where((p == 0) | (p == 7), p, p + 2 * lax.rem(p, 2) - 1)
        iq = jnp.where((q == 0) | (q == 3), q, q + 2 * lax.rem(q, 2) - 1)
        there = ip * NX + iq
        return pltpu.make_async_remote_copy(
            src_ref=part.at[slot], dst_ref=got.at[there],
            send_sem=r_send.at[slot], recv_sem=r_recv.at[there],
            device_id=device(lax.rem(x + dx, NX), y, lax.rem(z + dz, NZ), core),
            device_id_type=MESH,
        )

    def finish_tile(tile, total):
        for k in range(PER_TILE):
            slot = tile * PER_TILE + k
            block = total[:, k * VOWN : (k + 1) * VOWN]
            at = vols[slot]
            moved = (
                (block[0:24] * at[0:1] + block[24:48] * at[1:2]) + block[48:72] * at[2:3]
            ) + block[72:96]
            part[slot] = jnp.concatenate([moved, block[96:104]], axis=0)

    def one_tile(tile, _):
        @pl.when(tile > 0)
        def _():
            for k in range(PER_TILE):
                reduce_copy((tile - 1) * PER_TILE + k).start()

        total = jnp.dot(blk[...], weights(tile), preferred_element_type=f32)
        finish_tile(tile, total)
        return 0

    lax.fori_loop(0, TILES, one_tile, 0)
    for k in range(PER_TILE - 1):
        reduce_copy((TILES - 1) * PER_TILE + k).start()

    total = part[V_SLOTS - 1]
    for slot in range(V_SLOTS - 1):
        landed(got.at[slot], r_recv.at[slot])
        total = total + got[slot]
    out_ref[...] = total[0:24] / total[24:25]

    for copy in pending:
        copy.wait_send()

    def sent(slot, _):
        reduce_copy(slot).wait_send()
        return 0

    lax.fori_loop(0, V_SLOTS - 1, sent, 0)


def on_device(surf_xyz, surf_disp, neighbours, vol_xyz):
    dma = pltpu.SemaphoreType.DMA
    vmem = pl.BlockSpec(memory_space=pltpu.VMEM)
    return pl.pallas_call(
        kernel,
        out_shape=jax.ShapeDtypeStruct((24, VOWN), f32),
        in_specs=[vmem] * 4,
        out_specs=vmem,
        scratch_shapes=[
            pltpu.VMEM((32, 128, 128), f32),
            pltpu.VMEM((8, OWN), f32),
            pltpu.VMEM((SET, 8, OWN), f32),
            pltpu.VMEM((8, VOWN), f32),
            pltpu.VMEM((V_SLOTS, 8, VOWN), f32),
            pltpu.VMEM((S_ALL, FEAT), bf16),
            pltpu.VMEM((FEAT, V_ALL), bf16),
            pltpu.VMEM((4, OWN, 128), f32),
            pltpu.VMEM((4, OWN), i32),
            pltpu.SMEM((4, OWN), i32),
            pltpu.VMEM((ROWS, OWN), bf16),
            pltpu.VMEM((ROWS, S_ALL), bf16),
            pltpu.VMEM((V_SLOTS, 32, VOWN), f32),
            pltpu.VMEM((V_SLOTS, 32, VOWN), f32),
            pltpu.VMEM((max(CACHED, 1), 8, 128) if not CACHED else (CACHED, S_ALL, TILE), bf16),
            dma((2,)), dma((2,)), dma((10, NX)), dma((10, NY)), dma((32, 2)),
            dma((2, NY)), dma((SET,)), dma((V_SLOTS,)), dma((V_SLOTS,)),
            dma((8,)), dma((SET,)), dma((V_SLOTS,)), dma((V_SLOTS,)), dma,
        ],
        compiler_params=pltpu.CompilerParams(
            collective_id=0, has_side_effects=True, vmem_limit_bytes=62 << 20
        ),
        name="warp",
    )(surf_xyz, surf_disp, neighbours, vol_xyz)


def solution(mesh):
    spec = P(None, ("blk", "wide"))
    return jax.shard_map(
        on_device, mesh=mesh, in_specs=(spec,) * 4, out_specs=spec, check_vma=False
    )
```

time: 811 us -> 80.5 us (0.10)
  blocking collectives: 288 us -> 0 us
  matrix products: 201 us -> 0 us
  waiting for transfers between devices: 143 us -> 0 us
  Pallas kernels: 0 us -> 78.9 us
  other arithmetic: 66.2 us -> 0 us
  local copies, waits for them, and re-layouts: 58.7 us -> 1.35 us
  starting transfers between devices: 28.1 us -> 0 us
  between operations: 13.9 us -> 0.01 us
    all_gather x1 -> x0, blocking collectives: 288 us -> none  [on_device(): lax.all_gather(surf_xyz, 'wide', axis=1, tiled=True)]
    dot_general x128 -> x0, matrix products: 201 us -> none  [one_piece(): jnp.dot(block_piece, weights, preferred_element_type=jnp.float32)]
    all_gather x2 -> x0, waiting for transfers between devices: 126 us -> none  [the longest x1 126 us: on_device(): blocks = lax.all_gather(own_blocks, 'wide', axis=1, tiled=True)]
    pallas_call x0 -> x1, Pallas kernels: none -> 78.9 us  [on_device(): pl.pallas_call(kernel, out_shape=jax.ShapeDtypeStruct((24, VOWN), f32), i...]
    reduce_sum x128 -> x0, other arithmetic: 64.1 us -> none  [one_piece(): partial_den = partial_den + jnp.sum(weights.astype(jnp.float32), axis=0)]
    gather x12 -> x0, local copies, waits for them, and re-layouts: 35.7 us -> none  [the longest x2 4.52 us: form_blocks(): jnp.take(source_xyz, links[2], axis=1)]
    ppermute x23 -> x0, starting transfers between devices: 28.1 us -> none  [from_behind(): lax.ppermute(shard, axis, [(i, (i + by) % peers) for i in range(peers)])]
    ppermute x23 -> x0, waiting for transfers between devices: 16.9 us -> none  [from_behind(): lax.ppermute(shard, axis, [(i, (i + by) % peers) for i in range(peers)])]
  transfers between devices with their start and end apart: 25 -> 0, of which waited for: 11 -> 0; matrix products, arithmetic and copies ran while one was open for 3% -> 0% of each run, Pallas kernels for 0% -> 0%
where the time goes in v1:
time: 80.5 us; the launch traced here: 80.3 us
  Pallas kernels  78.9 us (98%)
  local copies, waits for them, and re-layouts  1.35 us (2%)
    pallas_call x1, Pallas kernels, on_device(): pl.pallas_call(kernel, out_shape=jax.ShapeDtypeStruct((24, VOWN), f32), i...  78.9 us

profile of v1, /device:TPU:1, one launch (start us, length us, event | category | flops | bytes accessed | tf_op | source)
XLA Modules:
  0.0 80.3 jit_solution(3643301627235191448)
XLA Ops:
  0.0 78.9 %warp.1 = f32[24,256]{1,0:T(8,128)} custom-call(f32[3,512]{1,0:T(4,128)} %xyz_ref.1, f32[24,512]{1,0:T(8,128)} %disp_ref.1, s32[4,512]{1,0:T(4,128)} %near_ref.1, f32[3,256]{1,0:T(4,128)} %vol_ref.1), custom_call_target="tpu_custom_call" | custom-call | tf_op jit(solution)/shard_map/warp/pallas_call | solution.py:337
  78.9 1.3 %copy.6 = f32[24,256]{1,0:T(8,128)} copy(f32[24,256]{1,0:T(8,128)} %warp.1) | data formatting | bytes 49152

commit v2 on v1

v2 whole, which is shorter than its diff:
```python
import jax
import jax.numpy as jnp
from jax import lax
from jax.experimental import pallas as pl
from jax.experimental.pallas import tpu as pltpu
from jax.sharding import PartitionSpec as P

MESH = pl.DeviceIdType.MESH
tangent_floor = 0.04
core_radius = 0.04
f32, bf16, i32 = jnp.float32, jnp.bfloat16, jnp.int32

NX, NY, NZ = 4, 4, 8
LOW = 4
OWN = 512
VOWN = 256
TILE = 512
SET = 8
S_ALL = SET * OWN
V_SLOTS = NX * NZ
V_ALL = V_SLOTS * VOWN
PER_TILE = TILE // VOWN
TILES = V_ALL // TILE
ROWS = 104
FEAT = 32
CACHED = 12
EARLY = 8
RELAY_AT = (0, 1, 3)
BLOCKS_AT = 10
LAG = 3


def device(x, y, z, core):
    return (lax.rem(z, LOW) * 2 + core, (x * 2 + lax.div(z, LOW)) * NY + y)


def z_offset(p):
    if isinstance(p, int):
        return 4 + (1 - 2 * (p % 2)) * ((p + 1) // 2)
    return 4 + (1 - 2 * lax.rem(p, 2)) * lax.div(p + 1, 2)


def split(value):
    high = value.astype(bf16).astype(f32)
    rest = value - high
    middle = rest.astype(bf16).astype(f32)
    return high, middle, (rest - middle).astype(bf16).astype(f32)


PAIRS = ((0, 0), (0, 1), (1, 0), (0, 2), (2, 0), (1, 1), (1, 2), (2, 1))


def feature_rows(xyz, surface):
    count = xyz.shape[1]
    ones = jnp.ones((1, count), f32)
    rows = []
    scale = 1.0 if surface else -2.0
    norm = (xyz[0:1] * xyz[0:1] + xyz[1:2] * xyz[1:2]) + xyz[2:3] * xyz[2:3]
    for axis in range(3):
        parts = split(xyz[axis : axis + 1] * scale)
        rows += [parts[pair[0] if surface else pair[1]] for pair in PAIRS]
    if surface:
        rows += list(split(norm + core_radius)) + [ones] * 3
    else:
        rows += [ones] * 3 + list(split(norm))
    rows += [jnp.zeros((1, count), f32)] * (FEAT - len(rows))
    return jnp.concatenate(rows, axis=0)


def kernel(
    xyz_ref, disp_ref, near_ref, vol_ref, out_ref,
    tab, own_xyz, set_xyz, vols, fs, fv, picked, near_rows, near_smem,
    own_blk, blk, part, got_x, mid, got_z, cache,
    z_send, x_send, y_send, chunk_recv, sx_send, sx_recv, vx_send, vx_recv,
    vz_send, vz_recv, b_send, b_recv, rx_send, rx_recv, rz_send, rz_recv, local_sem,
):
    blk_id, wide_id = lax.axis_index("blk"), lax.axis_index("wide")
    core = lax.rem(blk_id, 2)
    z_low = lax.div(blk_id, 2)
    y = lax.rem(wide_id, NY)
    z_high = lax.rem(lax.div(wide_id, NY), 2)
    x = lax.div(wide_id, NY * 2)
    z = z_high * LOW + z_low
    other = 1 - core
    wide_at = lambda ax, ah, ay: (ax * 2 + ah) * NY + ay
    xs = [lax.rem(x + d, NX) for d in range(NX)]
    ys = [lax.rem(y + d, NY) for d in range(NY)]
    zs = [lax.rem(z + d, NZ) for d in range(NZ)]
    far_h = 1 - z_high
    x_peer = lambda d: device(xs[d], y, z, core)
    y_peer = lambda d: device(x, ys[d], z, core)
    z_peer = lambda d: device(x, y, zs[d], core)

    barrier = pltpu.get_barrier_semaphore()
    peers = [z_peer(4)] + [x_peer(d) for d in range(1, NX)]
    peers += [y_peer(d) for d in range(1, NY)]
    peers += [z_peer(d) for d in (3, 5, 2, 6, 1, 7)]
    peers += [device(x, ys[d], z, other) for d in range(NY)]
    for peer in peers:
        pl.semaphore_signal(barrier, inc=1, device_id=peer, device_id_type=MESH)

    xyz = xyz_ref[...]
    disp = disp_ref[...]
    zeros5 = jnp.zeros((5, OWN), f32)
    table = jnp.concatenate([disp, xyz, zeros5], axis=0)
    stacked = jnp.concatenate(
        [table[:, q * 128 : (q + 1) * 128] for q in range(4)], axis=0
    )
    tab[wide_id] = stacked.T
    own_xyz[0:3, :] = xyz
    vol = vol_ref[...]
    for h in range(2):
        vols[z, x, 3 * h : 3 * h + 3, :] = vol[:, h * 128 : (h + 1) * 128]
    near = near_ref[...]
    near_rows[...] = (near // OWN) * 128 + (near & 127)
    to_smem = pltpu.make_async_copy(near_rows, near_smem, local_sem)

    pl.semaphore_wait(barrier, len(peers))
    to_smem.start()

    def send(src, dst, send_sem, recv_sem, peer):
        copy = pltpu.make_async_remote_copy(
            src_ref=src, dst_ref=dst, send_sem=send_sem, recv_sem=recv_sem,
            device_id=peer, device_id_type=MESH,
        )
        copy.start()

    half = lambda w, h: tab.at[w, pl.ds(h * 64, 64), :]

    def landed(ref, sem):
        pltpu.make_async_copy(ref, ref, sem).wait()

    def send_x(w, h, number):
        for d in (1, 3, 2):
            send(half(w, h), half(w, h), x_send.at[number, d], chunk_recv.at[w, h], x_peer(d))

    def send_y(w, h, number):
        for d in (1, 3, 2):
            send(half(w, h), half(w, h), y_send.at[number, d], chunk_recv.at[w, h], y_peer(d))

    for h in range(2):
        send(half(wide_id, h), half(wide_id, h), z_send.at[h],
             chunk_recv.at[wide_id, h], z_peer(4))
    member = core * NY + y
    for d in range(1, NX):
        send(vols.at[z, x], vols.at[z, x], vx_send.at[d], vx_recv.at[x], x_peer(d))
    for c in range(2):
        for d in range(NY):
            if c or d:
                send(own_xyz, set_xyz.at[member], sx_send.at[c, d], sx_recv.at[member],
                     device(x, ys[d], z, core if c == 0 else other))
    send_x(wide_id, 0, 0)
    send_y(wide_id, 1, 0)
    send_y(wide_id, 0, 1)
    send_x(wide_id, 1, 1)

    for d in range(1, NX):
        landed(vols.at[z, xs[d]], vx_recv.at[xs[d]])
    for d in (4, 3, 5, 2, 6, 1, 7):
        send(vols.at[z], vols.at[z], vz_send.at[d], vz_recv.at[z], z_peer(d))

    set_xyz[member] = own_xyz[...]
    for c in range(2):
        for d in range(NY):
            who = (core if c == 0 else other) * NY + ys[d]
            if c or d:
                landed(set_xyz.at[who], sx_recv.at[who])
            rows = feature_rows(set_xyz[who], True)
            at = pl.multiple_of(who * OWN, OWN)
            fs[pl.ds(at, OWN), :] = rows.T.astype(bf16)

    for d in (0, 1, 7, 6, 2, 5, 3, 4):
        if d:
            landed(vols.at[zs[d]], vz_recv.at[zs[d]])
        parts = [vols[zs[d], k] for k in range(NX)]
        at_z = jnp.concatenate(
            [p[3 * h : 3 * h + 3] for p in parts for h in range(2)], axis=1
        )
        at = pl.multiple_of(zs[d] * (NX * VOWN), NX * VOWN)
        fv[:, pl.ds(at, NX * VOWN)] = feature_rows(at_z, False).astype(bf16)

    def place(order):
        p = lax.div(order, 2)
        z_to = lax.rem(z + z_offset(p), NZ)
        pair = lax.rem(lax.div(x, 2) + 1 + order, 2)
        return z_to, pair * 2

    def weights(order):
        z_to, x_to = place(order)
        at = pl.multiple_of((z_to * NX + x_to) * VOWN, TILE)
        radius = jnp.dot(fs[...], fv[:, pl.ds(at, TILE)], preferred_element_type=f32)
        return (1.0 / (radius * radius)).astype(bf16)

    def relay_near():
        for n, d in enumerate((1, 3, 2)):
            w = wide_at(xs[d], z_high, y)
            landed(half(w, 0), chunk_recv.at[w, 0])
            send_y(w, 0, 4 + n)
            w = wide_at(x, z_high, ys[d])
            landed(half(w, 1), chunk_recv.at[w, 1])
            send_x(w, 1, 4 + n)

    def start_far():
        far_w = wide_at(x, far_h, y)
        for h in range(2):
            landed(half(far_w, h), chunk_recv.at[far_w, h])
        send_x(far_w, 0, 2)
        send_y(far_w, 1, 2)
        send_y(far_w, 0, 3)
        send_x(far_w, 1, 3)

    def relay_far():
        for n, d in enumerate((1, 3, 2)):
            w = wide_at(xs[d], far_h, y)
            landed(half(w, 0), chunk_recv.at[w, 0])
            send_y(w, 0, 7 + n)
            w = wide_at(x, far_h, ys[d])
            landed(half(w, 1), chunk_recv.at[w, 1])
            send_x(w, 1, 7 + n)

    steps = dict(zip(RELAY_AT, (relay_near, start_far, relay_far)))

    def early(i, _):
        for at, step in steps.items():
            pl.when(i == at)(step)
        cache[CACHED - 1 - i] = weights(CACHED - 1 - i)
        return 0

    lax.fori_loop(0, EARLY, early, 0)

    for high in (z_high, far_h):
        for d in range(1, NX):
            for e in range(1, NY):
                w = wide_at(xs[d], high, ys[e])
                for h in range(2):
                    landed(half(w, h), chunk_recv.at[w, h])
        for d in range(1, NX):
            w = wide_at(xs[d], high, y)
            landed(half(w, 1), chunk_recv.at[w, 1])
            w = wide_at(x, high, ys[d])
            landed(half(w, 0), chunk_recv.at[w, 0])

    to_smem.wait()
    STEP = 8

    def pick(group, _):
        for k in range(STEP):
            j = group * STEP + k
            for n in range(4):
                row = near_smem[n, j]
                picked[n, pl.ds(j, 1), :] = tab[lax.div(row, 128), pl.ds(lax.rem(row, 128), 1), :]
        return 0

    lax.fori_loop(0, OWN // STEP, pick, 0)

    chosen = []
    for n in range(4):
        quarter = lax.rem(lax.div(near[n : n + 1], 128), 4)
        turned = picked[n].T
        value = turned[0:32]
        for q in range(1, 4):
            value = jnp.where(quarter == q, turned[q * 32 : (q + 1) * 32], value)
        chosen.append(value)
    first, second = chosen[0] - chosen[1], chosen[2] - chosen[3]

    def scaled(change):
        t = change[24:27]
        length = (t[0:1] * t[0:1] + t[1:2] * t[1:2]) + t[2:3] * t[2:3]
        return t / (length + tangent_floor)

    one, two = scaled(first), scaled(second)
    linear = [
        first[0:24] * one[q : q + 1] + second[0:24] * two[q : q + 1] for q in range(3)
    ]
    offset = (linear[0] * xyz[0:1] + linear[1] * xyz[1:2]) + linear[2] * xyz[2:3]
    tail = jnp.where(lax.broadcasted_iota(i32, (8, OWN), 0) == 0, 1.0, 0.0)
    own_blk[...] = jnp.concatenate(linear + [disp - offset, tail], axis=0).astype(bf16)

    def columns(who):
        return blk.at[:, pl.ds(pl.multiple_of(who * OWN, OWN), OWN)]

    own_copy = pltpu.make_async_copy(own_blk, columns(member), local_sem)
    own_copy.start()
    for d in (2, 1, 3):
        send(own_blk, columns(member), b_send.at[d], b_recv.at[member], y_peer(d))
    send(own_blk, columns(member), b_send.at[0], b_recv.at[member],
         device(x, y, z, other))
    own_copy.wait()

    def relay_blocks():
        for d in (1, 3, 2):
            who = core * NY + ys[d]
            landed(columns(who), b_recv.at[who])
            send(columns(who), columns(who), b_send.at[3 + d], b_recv.at[who],
                 device(x, y, z, other))

    def late(i, _):
        cache[CACHED - 1 - i] = weights(CACHED - 1 - i)
        pl.when(i == BLOCKS_AT)(relay_blocks)
        return 0

    lax.fori_loop(EARLY, CACHED, late, 0)

    for d in range(NY):
        who = other * NY + ys[d]
        landed(columns(who), b_recv.at[who])

    def x_copy(p, d):
        z_to = lax.rem(z + z_offset(p), NZ)
        return pltpu.make_async_remote_copy(
            src_ref=part.at[z_to, xs[d]], dst_ref=got_x.at[z_to, x],
            send_sem=rx_send.at[z_to, d], recv_sem=rx_recv.at[z_to, x],
            device_id=x_peer(d), device_id_type=MESH,
        )

    def z_copy(p):
        z_to = lax.rem(z + z_offset(p), NZ)
        return pltpu.make_async_remote_copy(
            src_ref=mid.at[z_to], dst_ref=got_z.at[z],
            send_sem=rz_send.at[z_to], recv_sem=rz_recv.at[z],
            device_id=device(x, y, z_to, core), device_id_type=MESH,
        )

    def collect(p):
        z_to = lax.rem(z + z_offset(p), NZ)
        total = part[z_to, x]
        for d in range(1, NX):
            landed(got_x.at[z_to, xs[d]], rx_recv.at[z_to, xs[d]])
            total = total + got_x[z_to, xs[d]]
        mid[z_to] = total

    def traffic(order):
        p = lax.div(order, 2)

        @pl.when(lax.rem(order, 2) == 0)
        def _():
            @pl.when(p >= 1)
            def _():
                for d in (2, 1, 3):
                    x_copy(p - 1, d).start()

            @pl.when(p >= LAG + 1)
            def _():
                z_copy(p - LAG - 1).start()

            @pl.when(p >= LAG)
            def _():
                collect(p - LAG)

    def finish_tile(order, weight):
        total = jnp.dot(blk[...], weight, preferred_element_type=f32)
        z_to, x_to = place(order)
        for k in range(PER_TILE):
            block = total[:, k * VOWN : (k + 1) * VOWN]
            raw = vols[z_to, x_to + k]
            at = jnp.concatenate([raw[0:3], raw[3:6]], axis=1)
            moved = (
                (block[0:24] * at[0:1] + block[24:48] * at[1:2]) + block[48:72] * at[2:3]
            ) + block[72:96]
            part[z_to, x_to + k] = jnp.concatenate([moved, block[96:104]], axis=0)

    def cached_tile(order, _):
        traffic(order)
        finish_tile(order, cache[order])
        return 0

    def fresh_tile(order, _):
        traffic(order)
        finish_tile(order, weights(order))
        return 0

    lax.fori_loop(0, CACHED, cached_tile, 0)
    lax.fori_loop(CACHED, TILES, fresh_tile, 0)

    for d in (2, 1, 3):
        x_copy(NZ - 1, d).start()
    for p in range(NZ - LAG, NZ):
        if p - 1 >= 0:
            z_copy(p - 1).start()
        collect(p)
    total = mid[z]
    for d in range(1, NZ):
        landed(got_z.at[zs[d]], rz_recv.at[zs[d]])
        total = total + got_z[zs[d]]
    out_ref[...] = total[0:24] / total[24:25]

    for h in range(2):
        landed(half(0, 0), z_send.at[h])
    for d in range(1, NX):
        landed(vols.at[0, 0], vx_send.at[d])
        for number in range(10):
            landed(half(0, 0), x_send.at[number, d])
            landed(half(0, 0), y_send.at[number, d])
    for d in range(1, NZ):
        landed(vols.at[0], vz_send.at[d])
    for c in range(2):
        for d in range(NY):
            if c or d:
                landed(own_xyz, sx_send.at[c, d])
    for number in range(7):
        landed(own_blk, b_send.at[number])
    for p in range(NZ):
        for d in range(1, NX):
            x_copy(p, d).wait_send()
        if p < NZ - 1:
            z_copy(p).wait_send()


def on_device(surf_xyz, surf_disp, neighbours, vol_xyz):
    dma = pltpu.SemaphoreType.DMA
    vmem = pl.BlockSpec(memory_space=pltpu.VMEM)
    return pl.pallas_call(
        kernel,
        out_shape=jax.ShapeDtypeStruct((24, VOWN), f32),
        in_specs=[vmem] * 4,
        out_specs=vmem,
        scratch_shapes=[
            pltpu.VMEM((32, 128, 128), f32),
            pltpu.VMEM((8, OWN), f32),
            pltpu.VMEM((SET, 8, OWN), f32),
            pltpu.VMEM((NZ, NX, 8, 128), f32),
            pltpu.VMEM((S_ALL, FEAT), bf16),
            pltpu.VMEM((FEAT, V_ALL), bf16),
            pltpu.VMEM((4, OWN, 128), f32),
            pltpu.VMEM((4, OWN), i32),
            pltpu.SMEM((4, OWN), i32),
            pltpu.VMEM((ROWS, OWN), bf16),
            pltpu.VMEM((ROWS, S_ALL), bf16),
            pltpu.VMEM((NZ, NX, 32, VOWN), f32),
            pltpu.VMEM((NZ, NX, 32, VOWN), f32),
            pltpu.VMEM((NZ, 32, VOWN), f32),
            pltpu.VMEM((NZ, 32, VOWN), f32),
            pltpu.VMEM((CACHED, S_ALL, TILE), bf16),
            dma((2,)), dma((10, NX)), dma((10, NY)), dma((32, 2)),
            dma((2, NY)), dma((SET,)), dma((NX,)), dma((NX,)),
            dma((NZ,)), dma((NZ,)), dma((8,)), dma((SET,)),
            dma((NZ, NX)), dma((NZ, NX)), dma((NZ,)), dma((NZ,)), dma,
        ],
        compiler_params=pltpu.CompilerParams(
            collective_id=0, has_side_effects=True, vmem_limit_bytes=67043328
        ),
        name="warp",
    )(surf_xyz, surf_disp, neighbours, vol_xyz)


def solution(mesh):
    spec = P(None, ("blk", "wide"))
    return jax.shard_map(
        on_device, mesh=mesh, in_specs=(spec,) * 4, out_specs=spec, check_vma=False
    )
```

time: 80.5 us -> 70.9 us (0.88)
  Pallas kernels: 78.9 us -> 69 us
    pallas_call x1, Pallas kernels: 78.9 us -> 69 us  [on_device(): pl.pallas_call(kernel, out_shape=jax.ShapeDtypeStruct((24, VOWN), f32), i...]
where the time goes in v2:
time: 70.9 us; the launch traced here: 70.3 us
  Pallas kernels  69 us (97%)
  local copies, waits for them, and re-layouts  1.35 us (2%)
    pallas_call x1, Pallas kernels, on_device(): pl.pallas_call(kernel, out_shape=jax.ShapeDtypeStruct((24, VOWN), f32), i...  69 us

profile of v2, /device:TPU:1, one launch (start us, length us, event | category | flops | bytes accessed | tf_op | source)
XLA Modules:
  0.0 70.3 jit_solution(14837533048753804423)
XLA Ops:
  0.0 69.0 %warp.1 = f32[24,256]{1,0:T(8,128)} custom-call(f32[3,512]{1,0:T(4,128)} %xyz_ref.1, f32[24,512]{1,0:T(8,128)} %disp_ref.1, s32[4,512]{1,0:T(4,128)} %near_ref.1, f32[3,256]{1,0:T(4,128)} %vol_ref.1), custom_call_target="tpu_custom_call" | custom-call | tf_op jit(solution)/shard_map/warp/pallas_call | solution.py:412
  69.0 1.3 %copy.6 = f32[24,256]{1,0:T(8,128)} copy(f32[24,256]{1,0:T(8,128)} %warp.1) | data formatting | bytes 49152

commit v3 on v2

v3 whole, which is shorter than its diff:
```python
import jax
import jax.numpy as jnp
from jax import lax
from jax.experimental import pallas as pl
from jax.experimental.pallas import tpu as pltpu
from jax.sharding import PartitionSpec as P

MESH = pl.DeviceIdType.MESH
tangent_floor = 0.04
core_radius = 0.04
f32, bf16, i32 = jnp.float32, jnp.bfloat16, jnp.int32

NX, NY, NZ = 4, 4, 8
LOW = 4
OWN = 512
VOWN = 256
TILE = 512
SET = 8
S_ALL = SET * OWN
V_SLOTS = NX * NZ
V_ALL = V_SLOTS * VOWN
PER_TILE = TILE // VOWN
TILES = V_ALL // TILE
ROWS = 104
FEAT = 32
CACHED = 9
EARLY = 5
RELAY_AT = 1
BLOCKS_AT = 7
LAG = 3


def device(x, y, z, core):
    return (lax.rem(z, LOW) * 2 + core, (x * 2 + lax.div(z, LOW)) * NY + y)


def z_offset(p):
    if isinstance(p, int):
        return 4 + (1 - 2 * (p % 2)) * ((p + 1) // 2)
    return 4 + (1 - 2 * lax.rem(p, 2)) * lax.div(p + 1, 2)


def split(value):
    high = value.astype(bf16).astype(f32)
    rest = value - high
    middle = rest.astype(bf16).astype(f32)
    return high, middle, (rest - middle).astype(bf16).astype(f32)


PAIRS = ((0, 0), (0, 1), (1, 0), (0, 2), (2, 0), (1, 1), (1, 2), (2, 1))


def feature_rows(xyz, surface):
    count = xyz.shape[1]
    ones = jnp.ones((1, count), f32)
    rows = []
    scale = 1.0 if surface else -2.0
    norm = (xyz[0:1] * xyz[0:1] + xyz[1:2] * xyz[1:2]) + xyz[2:3] * xyz[2:3]
    for axis in range(3):
        parts = split(xyz[axis : axis + 1] * scale)
        rows += [parts[pair[0] if surface else pair[1]] for pair in PAIRS]
    if surface:
        rows += list(split(norm + core_radius)) + [ones] * 3
    else:
        rows += [ones] * 3 + list(split(norm))
    rows += [jnp.zeros((1, count), f32)] * (FEAT - len(rows))
    return jnp.concatenate(rows, axis=0)


def kernel(
    xyz_ref, disp_ref, near_ref, vol_ref, out_ref,
    tab, own_xyz, set_xyz, vols, fs, fv, picked, near_rows, near_smem,
    own_blk, blk, part, got_x, mid, got_z, cache,
    chunk_send, near_recv, far_recv, twin_recv, rest_recv, sx_send, sx_recv,
    vx_send, vx_recv, vz_send, vz_recv, b_send, b_recv, sibling_recv,
    rx_send, rx_recv, rz_send, rz_recv, local_sem,
):
    blk_id, wide_id = lax.axis_index("blk"), lax.axis_index("wide")
    core = lax.rem(blk_id, 2)
    z_low = lax.div(blk_id, 2)
    y = lax.rem(wide_id, NY)
    z_high = lax.rem(lax.div(wide_id, NY), 2)
    x = lax.div(wide_id, NY * 2)
    z = z_high * LOW + z_low
    other = 1 - core
    wide_at = lambda ax, ah, ay: (ax * 2 + ah) * NY + ay
    xs = [lax.rem(x + d, NX) for d in range(NX)]
    ys = [lax.rem(y + d, NY) for d in range(NY)]
    zs = [lax.rem(z + d, NZ) for d in range(NZ)]
    far_h = 1 - z_high
    x_peer = lambda d: device(xs[d], y, z, core)
    y_peer = lambda d: device(x, ys[d], z, core)
    z_peer = lambda d: device(x, y, zs[d], core)

    barrier = pltpu.get_barrier_semaphore()
    peers = [z_peer(4)] + [x_peer(d) for d in range(1, NX)]
    peers += [y_peer(d) for d in range(1, NY)]
    peers += [z_peer(d) for d in (3, 5, 2, 6, 1, 7)]
    peers += [device(x, ys[d], z, other) for d in range(NY)]
    for peer in peers:
        pl.semaphore_signal(barrier, inc=1, device_id=peer, device_id_type=MESH)

    xyz = xyz_ref[...]
    disp = disp_ref[...]
    zeros5 = jnp.zeros((5, OWN), f32)
    table = jnp.concatenate([disp, xyz, zeros5], axis=0)
    stacked = jnp.concatenate(
        [table[:, q * 128 : (q + 1) * 128] for q in range(4)], axis=0
    )
    tab[pl.ds(pl.multiple_of(wide_id * 128, 128), 128), :] = stacked.T
    own_xyz[0:3, :] = xyz
    vol = vol_ref[...]
    for h in range(2):
        vols[z, x, 3 * h : 3 * h + 3, :] = vol[:, h * 128 : (h + 1) * 128]
    near = near_ref[...]
    near_rows[...] = (near // OWN) * 128 + (near & 127)
    to_smem = pltpu.make_async_copy(near_rows, near_smem, local_sem.at[0])

    pl.semaphore_wait(barrier, len(peers))
    to_smem.start()

    def send(src, dst, send_sem, recv_sem, peer):
        copy = pltpu.make_async_remote_copy(
            src_ref=src, dst_ref=dst, send_sem=send_sem, recv_sem=recv_sem,
            device_id=peer, device_id_type=MESH,
        )
        copy.start()

    half = lambda w, h: tab.at[pl.ds(pl.multiple_of(w * 128 + h * 64, 64), 64), :]

    def landed(ref, sem):
        pltpu.make_async_copy(ref, ref, sem).wait()

    def send_x(w, h, recv=None):
        for d in (1, 3, 2):
            sem = rest_recv if recv is None else recv.at[0, NX - d]
            send(half(w, h), half(w, h), chunk_send, sem, x_peer(d))

    def send_y(w, h, recv=None):
        for d in (1, 3, 2):
            sem = rest_recv if recv is None else recv.at[1, NY - d]
            send(half(w, h), half(w, h), chunk_send, sem, y_peer(d))

    for h in range(2):
        send(half(wide_id, h), half(wide_id, h), chunk_send, twin_recv, z_peer(4))
    member = core * NY + y
    for d in range(1, NX):
        send(vols.at[z, x], vols.at[z, x], vx_send, vx_recv, x_peer(d))
    send_x(wide_id, 0, near_recv)
    send_y(wide_id, 1, near_recv)
    for c in range(2):
        for d in range(NY):
            if c or d:
                send(own_xyz, set_xyz.at[member], sx_send, sx_recv,
                     device(x, ys[d], z, core if c == 0 else other))
    send_y(wide_id, 0)
    send_x(wide_id, 1)
    set_xyz[member] = own_xyz[...]

    landed(vols.at[0, pl.ds(0, NX - 1)], vx_recv)
    for d in (4, 3, 5, 2, 6, 1, 7):
        send(vols.at[z], vols.at[z], vz_send, vz_recv, z_peer(d))

    def relay_near():
        for d in (1, 3, 2):
            w = wide_at(xs[d], z_high, y)
            landed(half(w, 0), near_recv.at[0, d])
            send_y(w, 0)
            w = wide_at(x, z_high, ys[d])
            landed(half(w, 1), near_recv.at[1, d])
            send_x(w, 1)

    def start_far():
        far_w = wide_at(x, far_h, y)
        landed(tab.at[pl.ds(pl.multiple_of(far_w * 128, 128), 128), :], twin_recv)
        send_x(far_w, 0, far_recv)
        send_y(far_w, 1, far_recv)
        send_y(far_w, 0)
        send_x(far_w, 1)

    def relay_far():
        for d in (1, 3, 2):
            w = wide_at(xs[d], far_h, y)
            landed(half(w, 0), far_recv.at[0, d])
            send_y(w, 0)
            w = wide_at(x, far_h, ys[d])
            landed(half(w, 1), far_recv.at[1, d])
            send_x(w, 1)

    relay_near()

    landed(set_xyz.at[pl.ds(0, SET - 1)], sx_recv)
    for who in range(SET):
        rows = feature_rows(set_xyz[who], True)
        fs[who * OWN : (who + 1) * OWN, :] = rows.T.astype(bf16)

    start_far()

    landed(vols.at[pl.ds(0, NZ - 1)], vz_recv)
    for k in range(NZ):
        parts = [vols[k, j] for j in range(NX)]
        at_z = jnp.concatenate(
            [p[3 * h : 3 * h + 3] for p in parts for h in range(2)], axis=1
        )
        width = NX * VOWN
        fv[:, k * width : (k + 1) * width] = feature_rows(at_z, False).astype(bf16)

    def place(order):
        p = lax.div(order, 2)
        z_to = lax.rem(z + z_offset(p), NZ)
        pair = lax.rem(lax.div(x, 2) + 1 + order, 2)
        return z_to, pair * 2

    def weights(order):
        z_to, x_to = place(order)
        at = pl.multiple_of((z_to * NX + x_to) * VOWN, TILE)
        radius = jnp.dot(fs[...], fv[:, pl.ds(at, TILE)], preferred_element_type=f32)
        return (1.0 / (radius * radius)).astype(bf16)

    def early(i, _):
        pl.when(i == RELAY_AT)(relay_far)
        cache[CACHED - 1 - i] = weights(CACHED - 1 - i)
        return 0

    lax.fori_loop(0, EARLY, early, 0)

    landed(tab.at[pl.ds(0, 24 * 128), :], rest_recv)

    to_smem.wait()
    STEP = 16
    PART = OWN // 2

    def pick(group, _):
        for k in range(STEP):
            j = group * STEP + k
            for n in range(4):
                picked[n, pl.ds(j, 1), :] = tab[pl.ds(near_smem[n, j], 1), :]
        return 0

    def scaled(change):
        t = change[24:27]
        length = (t[0:1] * t[0:1] + t[1:2] * t[1:2]) + t[2:3] * t[2:3]
        return t / (length + tangent_floor)

    def columns(who, h=None):
        at = who * OWN + (h or 0) * PART
        size = OWN if h is None else PART
        return blk.at[:, pl.ds(pl.multiple_of(at, PART), size)]

    def build(h):
        at = slice(h * PART, (h + 1) * PART)
        chosen = []
        for n in range(4):
            quarter = lax.rem(lax.div(near[n : n + 1, at], 128), 4)
            turned = picked[n, at].T
            value = turned[0:32]
            for q in range(1, 4):
                value = jnp.where(quarter == q, turned[q * 32 : (q + 1) * 32], value)
            chosen.append(value)
        first, second = chosen[0] - chosen[1], chosen[2] - chosen[3]
        one, two = scaled(first), scaled(second)
        linear = [
            first[0:24] * one[q : q + 1] + second[0:24] * two[q : q + 1]
            for q in range(3)
        ]
        place_y = xyz[:, at]
        offset = (
            linear[0] * place_y[0:1] + linear[1] * place_y[1:2]
        ) + linear[2] * place_y[2:3]
        tail = jnp.where(lax.broadcasted_iota(i32, (8, PART), 0) == 0, 1.0, 0.0)
        own_blk[h] = jnp.concatenate(
            linear + [disp[:, at] - offset, tail], axis=0
        ).astype(bf16)

    own_copies = []
    for h in range(2):
        lax.fori_loop(h * PART // STEP, (h + 1) * PART // STEP, pick, 0)
        build(h)
        for d in (2, 1, 3):
            send(own_blk.at[h], columns(member, h), b_send, b_recv.at[NY - d], y_peer(d))
        send(own_blk.at[h], columns(member, h), b_send, sibling_recv,
             device(x, y, z, other))
        copy = pltpu.make_async_copy(own_blk.at[h], columns(member, h), local_sem.at[h])
        copy.start()
        own_copies.append(copy)

    for copy in own_copies:
        copy.wait()

    def relay_blocks():
        for d in (1, 3, 2):
            who = core * NY + ys[d]
            landed(columns(who), b_recv.at[d])
            send(columns(who), columns(who), b_send, sibling_recv,
                 device(x, y, z, other))

    def late(i, _):
        cache[CACHED - 1 - i] = weights(CACHED - 1 - i)
        pl.when(i == BLOCKS_AT)(relay_blocks)
        return 0

    lax.fori_loop(EARLY, CACHED, late, 0)

    landed(blk.at[:, pl.ds(0, NY * OWN)], sibling_recv)

    def x_copy(p, d):
        z_to = lax.rem(z + z_offset(p), NZ)
        return pltpu.make_async_remote_copy(
            src_ref=part.at[z_to, xs[d]], dst_ref=got_x.at[z_to, x],
            send_sem=rx_send, recv_sem=rx_recv.at[z_to],
            device_id=x_peer(d), device_id_type=MESH,
        )

    def z_copy(p):
        z_to = lax.rem(z + z_offset(p), NZ)
        return pltpu.make_async_remote_copy(
            src_ref=mid.at[z_to], dst_ref=got_z.at[z],
            send_sem=rz_send, recv_sem=rz_recv,
            device_id=device(x, y, z_to, core), device_id_type=MESH,
        )

    def collect(p):
        z_to = lax.rem(z + z_offset(p), NZ)
        total = part[z_to, x]
        landed(got_x.at[z_to, pl.ds(0, NX - 1)], rx_recv.at[z_to])
        for d in range(1, NX):
            total = total + got_x[z_to, xs[d]]
        mid[z_to] = total

    def traffic(order):
        p = lax.div(order, 2)

        @pl.when(lax.rem(order, 2) == 0)
        def _():
            @pl.when(p >= 1)
            def _():
                for d in (2, 1, 3):
                    x_copy(p - 1, d).start()

            @pl.when(p >= LAG + 1)
            def _():
                z_copy(p - LAG - 1).start()

            @pl.when(p >= LAG)
            def _():
                collect(p - LAG)

    def finish_tile(order, weight):
        total = jnp.dot(blk[...], weight, preferred_element_type=f32)
        z_to, x_to = place(order)
        for k in range(PER_TILE):
            block = total[:, k * VOWN : (k + 1) * VOWN]
            raw = vols[z_to, x_to + k]
            at = jnp.concatenate([raw[0:3], raw[3:6]], axis=1)
            moved = (
                (block[0:24] * at[0:1] + block[24:48] * at[1:2]) + block[48:72] * at[2:3]
            ) + block[72:96]
            part[z_to, x_to + k] = jnp.concatenate([moved, block[96:104]], axis=0)

    def cached_tile(order, _):
        traffic(order)
        finish_tile(order, cache[order])
        return 0

    def fresh_tile(order, _):
        traffic(order)
        finish_tile(order, weights(order))
        return 0

    lax.fori_loop(0, CACHED, cached_tile, 0)
    lax.fori_loop(CACHED, TILES, fresh_tile, 0)

    for d in (2, 1, 3):
        x_copy(NZ - 1, d).start()
    for p in range(NZ - LAG, NZ):
        if p - 1 >= 0:
            z_copy(p - 1).start()
        collect(p)
    total = mid[z]
    landed(got_z.at[pl.ds(0, NZ - 1)], rz_recv)
    for d in range(1, NZ):
        total = total + got_z[zs[d]]
    out_ref[...] = total[0:24] / total[24:25]

    landed(tab.at[pl.ds(0, 31 * 128), :], chunk_send)
    landed(vols.at[0, pl.ds(0, NX - 1)], vx_send)
    landed(vols.at[pl.ds(0, NZ - 1)], vz_send)
    landed(set_xyz.at[pl.ds(0, SET - 1)], sx_send)
    landed(blk.at[:, pl.ds(0, 7 * OWN)], b_send)
    landed(part.at[:, pl.ds(0, NX - 1)], rx_send)
    landed(mid.at[pl.ds(0, NZ - 1)], rz_send)


def on_device(surf_xyz, surf_disp, neighbours, vol_xyz):
    dma = pltpu.SemaphoreType.DMA
    vmem = pl.BlockSpec(memory_space=pltpu.VMEM)
    return pl.pallas_call(
        kernel,
        out_shape=jax.ShapeDtypeStruct((24, VOWN), f32),
        in_specs=[vmem] * 4,
        out_specs=vmem,
        scratch_shapes=[
            pltpu.VMEM((32 * 128, 128), f32),
            pltpu.VMEM((8, OWN), f32),
            pltpu.VMEM((SET, 8, OWN), f32),
            pltpu.VMEM((NZ, NX, 8, 128), f32),
            pltpu.VMEM((S_ALL, FEAT), bf16),
            pltpu.VMEM((FEAT, V_ALL), bf16),
            pltpu.VMEM((4, OWN, 128), f32),
            pltpu.VMEM((4, OWN), i32),
            pltpu.SMEM((4, OWN), i32),
            pltpu.VMEM((2, ROWS, OWN // 2), bf16),
            pltpu.VMEM((ROWS, S_ALL), bf16),
            pltpu.VMEM((NZ, NX, 32, VOWN), f32),
            pltpu.VMEM((NZ, NX, 32, VOWN), f32),
            pltpu.VMEM((NZ, 32, VOWN), f32),
            pltpu.VMEM((NZ, 32, VOWN), f32),
            pltpu.VMEM((CACHED, S_ALL, TILE), bf16),
            dma, dma((2, NX)), dma((2, NX)), dma, dma, dma, dma,
            dma, dma, dma, dma, dma, dma((NY,)), dma,
            dma, dma((NZ,)), dma, dma, dma((2,)),
        ],
        compiler_params=pltpu.CompilerParams(
            collective_id=0, has_side_effects=True, vmem_limit_bytes=67043328
        ),
        name="warp",
    )(surf_xyz, surf_disp, neighbours, vol_xyz)


def solution(mesh):
    spec = P(None, ("blk", "wide"))
    return jax.shard_map(
        on_device, mesh=mesh, in_specs=(spec,) * 4, out_specs=spec, check_vma=False
    )
```

time: 70.9 us -> 64.1 us (0.904)
  Pallas kernels: 69 us -> 62.6 us
    pallas_call x1, Pallas kernels: 69 us -> 62.6 us  [on_device(): pl.pallas_call(kernel, out_shape=jax.ShapeDtypeStruct((24, VOWN), f32), i...]
where the time goes in v3:
time: 64.1 us; the launch traced here: 63.9 us
  Pallas kernels  62.6 us (98%)
  local copies, waits for them, and re-layouts  1.35 us (2%)
    pallas_call x1, Pallas kernels, on_device(): pl.pallas_call(kernel, out_shape=jax.ShapeDtypeStruct((24, VOWN), f32), i...  62.6 us
    unnamed x1, local copies, waits for them, and re-layouts  1.35 us

profile of v3, /device:TPU:1, one launch (start us, length us, event | category | flops | bytes accessed | tf_op | source)
XLA Modules:
  0.0 63.9 jit_solution(697677736053872306)
XLA Ops:
  0.0 62.6 %warp.1 = f32[24,256]{1,0:T(8,128)} custom-call(f32[3,512]{1,0:T(4,128)} %xyz_ref.1, f32[24,512]{1,0:T(8,128)} %disp_ref.1, s32[4,512]{1,0:T(4,128)} %near_ref.1, f32[3,256]{1,0:T(4,128)} %vol_ref.1), custom_call_target="tpu_custom_call" | custom-call | tf_op jit(solution)/shard_map/warp/pallas_call | solution.py:397
  62.6 1.3 %copy.6 = f32[24,256]{1,0:T(8,128)} copy(f32[24,256]{1,0:T(8,128)} %warp.1) | data formatting | bytes 49152

commit v4 on v3

--- a/solution.py
+++ b/solution.py
@@ -27,7 +27,7 @@
 EARLY = 5
 RELAY_AT = 1
 BLOCKS_AT = 7
-LAG = 3
+CHUNK = 4096
 
 
 def device(x, y, z, core):
@@ -113,7 +113,9 @@
     for h in range(2):
         vols[z, x, 3 * h : 3 * h + 3, :] = vol[:, h * 128 : (h + 1) * 128]
     near = near_ref[...]
-    near_rows[...] = (near // OWN) * 128 + (near & 127)
+    rows = (near // OWN) * 128 + (near & 127)
+    lines = [rows[:, b * 128 : (b + 1) * 128] for b in range(4)]
+    near_rows[...] = jnp.concatenate(lines + [jnp.zeros((112, 128), i32)], axis=0).T
     to_smem = pltpu.make_async_copy(near_rows, near_smem, local_sem.at[0])
 
     pl.semaphore_wait(barrier, len(peers))
@@ -146,13 +148,13 @@
     member = core * NY + y
     for d in range(1, NX):
         send(vols.at[z, x], vols.at[z, x], vx_send, vx_recv, x_peer(d))
-    send_x(wide_id, 0, near_recv)
-    send_y(wide_id, 1, near_recv)
     for c in range(2):
         for d in range(NY):
             if c or d:
                 send(own_xyz, set_xyz.at[member], sx_send, sx_recv,
                      device(x, ys[d], z, core if c == 0 else other))
+    send_x(wide_id, 0, near_recv)
+    send_y(wide_id, 1, near_recv)
     send_y(wide_id, 0)
     send_x(wide_id, 1)
     set_xyz[member] = own_xyz[...]
@@ -211,10 +213,12 @@
         pair = lax.rem(lax.div(x, 2) + 1 + order, 2)
         return z_to, pair * 2
 
-    def weights(order):
+    def weights(order, start=0, size=S_ALL):
         z_to, x_to = place(order)
         at = pl.multiple_of((z_to * NX + x_to) * VOWN, TILE)
-        radius = jnp.dot(fs[...], fv[:, pl.ds(at, TILE)], preferred_element_type=f32)
+        radius = jnp.dot(
+            fs[start : start + size, :], fv[:, pl.ds(at, TILE)], preferred_element_type=f32
+        )
         return (1.0 / (radius * radius)).astype(bf16)
 
     def early(i, _):
@@ -227,15 +231,17 @@
     landed(tab.at[pl.ds(0, 24 * 128), :], rest_recv)
 
     to_smem.wait()
-    STEP = 16
+    STEP = 8
     PART = OWN // 2
 
-    def pick(group, _):
+    def pick(h, group):
         for k in range(STEP):
-            j = group * STEP + k
-            for n in range(4):
-                picked[n, pl.ds(j, 1), :] = tab[pl.ds(near_smem[n, j], 1), :]
-        return 0
+            c = group * STEP + k
+            for b in (2 * h, 2 * h + 1):
+                for n in range(4):
+                    picked[n, pl.ds(b * 128 + c, 1), :] = tab[
+                        pl.ds(near_smem[c, 4 * b + n], 1), :
+                    ]
 
     def scaled(change):
         t = change[24:27]
@@ -274,7 +280,12 @@
 
     own_copies = []
     for h in range(2):
-        lax.fori_loop(h * PART // STEP, (h + 1) * PART // STEP, pick, 0)
+
+        def half_pick(group, _, h=h):
+            pick(h, group)
+            return 0
+
+        lax.fori_loop(0, 128 // STEP, half_pick, 0)
         build(h)
         for d in (2, 1, 3):
             send(own_blk.at[h], columns(member, h), b_send, b_recv.at[NY - d], y_peer(d))
@@ -303,13 +314,24 @@
 
     landed(blk.at[:, pl.ds(0, NY * OWN)], sibling_recv)
 
-    def x_copy(p, d):
-        z_to = lax.rem(z + z_offset(p), NZ)
+    def x_copy(z_to, x_to):
         return pltpu.make_async_remote_copy(
-            src_ref=part.at[z_to, xs[d]], dst_ref=got_x.at[z_to, x],
+            src_ref=part.at[z_to, x_to], dst_ref=got_x.at[z_to, x],
             send_sem=rx_send, recv_sem=rx_recv.at[z_to],
-            device_id=x_peer(d), device_id_type=MESH,
+            device_id=device(x_to, y, z, core), device_id_type=MESH,
         )
+
+    def pass_x(order):
+        z_to, x_to = place(order)
+
+        @pl.when(lax.rem(order, 2) == 0)
+        def _():
+            for k in range(PER_TILE):
+                x_copy(z_to, x_to + k).start()
+
+        @pl.when(lax.rem(order, 2) == 1)
+        def _():
+            x_copy(z_to, x_to + 1 - lax.rem(x, 2)).start()
 
     def z_copy(p):
         z_to = lax.rem(z + z_offset(p), NZ)
@@ -317,7 +339,7 @@
             src_ref=mid.at[z_to], dst_ref=got_z.at[z],
             send_sem=rz_send, recv_sem=rz_recv,
             device_id=device(x, y, z_to, core), device_id_type=MESH,
-        )
+        ).start()
 
     def collect(p):
         z_to = lax.rem(z + z_offset(p), NZ)
@@ -328,25 +350,30 @@
         mid[z_to] = total
 
     def traffic(order):
-        p = lax.div(order, 2)
-
-        @pl.when(lax.rem(order, 2) == 0)
-        def _():
-            @pl.when(p >= 1)
-            def _():
-                for d in (2, 1, 3):
-                    x_copy(p - 1, d).start()
-
-            @pl.when(p >= LAG + 1)
-            def _():
-                z_copy(p - LAG - 1).start()
-
-            @pl.when(p >= LAG)
-            def _():
-                collect(p - LAG)
-
-    def finish_tile(order, weight):
-        total = jnp.dot(blk[...], weight, preferred_element_type=f32)
+        even = lax.rem(order, 2) == 0
+        odd = lax.rem(order, 2) == 1
+
+        @pl.when(order >= 1)
+        def _():
+            pass_x(order - 1)
+
+        @pl.when(odd & (order >= 7) & (order <= 11))
+        def _():
+            z_copy(lax.div(order - 7, 2))
+
+        @pl.when(even & (order >= 12))
+        def _():
+            z_copy(lax.div(order - 6, 2))
+
+        @pl.when(even & (order >= 6) & (order <= 10))
+        def _():
+            collect(lax.div(order - 6, 2))
+
+        @pl.when(odd & (order >= 11))
+        def _():
+            collect(lax.div(order - 5, 2))
+
+    def finish_tile(order, total):
         z_to, x_to = place(order)
         for k in range(PER_TILE):
             block = total[:, k * VOWN : (k + 1) * VOWN]
@@ -359,23 +386,31 @@
 
     def cached_tile(order, _):
         traffic(order)
-        finish_tile(order, cache[order])
+        finish_tile(
+            order, jnp.dot(blk[...], cache[order], preferred_element_type=f32)
+        )
         return 0
 
     def fresh_tile(order, _):
         traffic(order)
-        finish_tile(order, weights(order))
+        total = jnp.zeros((ROWS, TILE), f32)
+        for at in range(0, S_ALL, CHUNK):
+            total = total + jnp.dot(
+                blk[:, at : at + CHUNK],
+                weights(order, at, CHUNK),
+                preferred_element_type=f32,
+            )
+        finish_tile(order, total)
         return 0
 
     lax.fori_loop(0, CACHED, cached_tile, 0)
     lax.fori_loop(CACHED, TILES, fresh_tile, 0)
 
-    for d in (2, 1, 3):
-        x_copy(NZ - 1, d).start()
-    for p in range(NZ - LAG, NZ):
-        if p - 1 >= 0:
-            z_copy(p - 1).start()
-        collect(p)
+    pass_x(TILES - 1)
+    z_copy(5)
+    collect(6)
+    z_copy(6)
+    collect(7)
     total = mid[z]
     landed(got_z.at[pl.ds(0, NZ - 1)], rz_recv)
     for d in range(1, NZ):
@@ -407,8 +442,8 @@
             pltpu.VMEM((S_ALL, FEAT), bf16),
             pltpu.VMEM((FEAT, V_ALL), bf16),
             pltpu.VMEM((4, OWN, 128), f32),
-            pltpu.VMEM((4, OWN), i32),
-            pltpu.SMEM((4, OWN), i32),
+            pltpu.VMEM((128, 128), i32),
+            pltpu.SMEM((128, 128), i32),
             pltpu.VMEM((2, ROWS, OWN // 2), bf16),
             pltpu.VMEM((ROWS, S_ALL), bf16),
             pltpu.VMEM((NZ, NX, 32, VOWN), f32),

time: 64.1 us -> 63.4 us (0.989)
  Pallas kernels: 62.6 us -> 61.8 us
    pallas_call x1, Pallas kernels: 62.6 us -> 61.8 us  [on_device(): pl.pallas_call(kernel, out_shape=jax.ShapeDtypeStruct((24, VOWN), f32), i...]
where the time goes in v4:
time: 63.4 us; the launch traced here: 63.2 us
  Pallas kernels  61.8 us (97%)
  local copies, waits for them, and re-layouts  1.35 us (2%)
    pallas_call x1, Pallas kernels, on_device(): pl.pallas_call(kernel, out_shape=jax.ShapeDtypeStruct((24, VOWN), f32), i...  61.8 us
    unnamed x1, local copies, waits for them, and re-layouts  1.35 us

profile of v4, /device:TPU:1, one launch (start us, length us, event | category | flops | bytes accessed | tf_op | source)
XLA Modules:
  0.0 63.2 jit_solution(16101872891506481548)
XLA Ops:
  0.0 61.8 %warp.1 = f32[24,256]{1,0:T(8,128)} custom-call(f32[3,512]{1,0:T(4,128)} %xyz_ref.1, f32[24,512]{1,0:T(8,128)} %disp_ref.1, s32[4,512]{1,0:T(4,128)} %near_ref.1, f32[3,256]{1,0:T(4,128)} %vol_ref.1), custom_call_target="tpu_custom_call" | custom-call | tf_op jit(solution)/shard_map/warp/pallas_call | solution.py:432
  61.8 1.3 %copy.6 = f32[24,256]{1,0:T(8,128)} copy(f32[24,256]{1,0:T(8,128)} %warp.1) | data formatting | bytes 49152
